TPU v7x, 256 devices: a whole 4x4x8 slice. The times are simulated.
256 devices in a mesh: seq: 32 (over y, z_lo, core), head: 8 (over x, z_hi).
Axes of the slice: x: 4, y: 4, z: 8 (z_hi: 2, z_lo: 4; z = z_hi * 4 + z_lo), core: 2. Of those that a mesh axis runs over, the one named last changes fastest.
Arguments:
- tokens: bfloat16 [131072, 1024], P(('seq', 'head')), may hold values from -32 to 32
- w_qkv: bfloat16 [1024, 3072], P('seq'), may hold values from -0.1875 to 0.1875
- w_out: bfloat16 [1024, 1024], P('seq'), may hold values from -0.1875 to 0.1875
- neighbours: int32 [1024, 12], P('seq'), may hold values from 0 to 1023, as said below
Outputs:
- update: bfloat16 [131072, 1024], P(('seq', 'head'))
Inputs may be any that keep to these rules, and one draw needn't show every extreme that they name: Block b has grid coordinates z = b // 16, y = (b // 4) % 4, x = b % 4. Each row lists b itself first, then 11 different blocks among its 26 neighbours at offsets -1, 0, 1 in each coordinate (z taken modulo 1024 // 16, y and x modulo 4).
All inputs are finite; a program needn't handle non-finite values.
Results may differ from a plain program's by a relative error of at most 0.0065.
The roundings to bfloat16 on the way count: a program that leaves them out, or rounds other values in their place, can miss the bound.
Values may be sent and summed in bfloat16 or wider, within the bound.
A program may use at most 64 MiB of HBM per device.

v0:
```python
import math
import jax
import jax.numpy as jnp
from jax import lax
from jax.sharding import PartitionSpec as P

HEADS = 8
HD = 128
BLK = 128
NBR = 12
PB = 16


def padded_2(cells, sides, width):
    for axis, dim in sides:
        count = lax.axis_size(axis)
        head = lax.slice_in_dim(cells, 0, width, axis=dim)
        tail = lax.slice_in_dim(cells, cells.shape[dim] - width, cells.shape[dim], axis=dim)
        cells = jnp.concatenate(
            [
                lax.ppermute(tail, axis, [(i, (i + 1) % count) for i in range(count)]),
                cells,
                lax.ppermute(head, axis, [((i + 1) % count, i) for i in range(count)]),
            ],
            axis=dim,
        )
    return cells


def local(tokens, w_qkv, w_out, neighbours):
    head_count = lax.axis_size("head")
    seq_count = lax.axis_size("seq")
    per_device = HEADS // head_count
    local_rows = tokens.shape[0]
    slab_rows = local_rows * head_count
    full_qkv = lax.all_gather(w_qkv, "seq", axis=0, tiled=True)
    projected = jnp.dot(tokens, full_qkv, preferred_element_type=jnp.float32)
    projected = projected.astype(jnp.bfloat16).reshape(local_rows, 3, HEADS, HD)
    slab = lax.all_to_all(projected, "head", split_axis=2, concat_axis=0, tiled=True)
    queries = slab[:, 0]
    key_value = slab[:, 1:3]
    padded = padded_2(key_value, (("seq", 0),), PB * BLK)
    kv_blocks = padded.reshape(-1, BLK, 2, per_device, HD)
    block_count = neighbours.shape[0]
    first_block = lax.axis_index("seq") * block_count
    local_lists = jnp.mod(neighbours - first_block + PB, block_count * seq_count)
    group_blocks = 4
    scale = 1.0 / math.sqrt(HD)

    def attend(args):
        query_group, list_group = args
        picked = kv_blocks[list_group].reshape(group_blocks, NBR * BLK, 2, per_device, HD)
        keys = picked[:, :, 0]
        values = picked[:, :, 1]
        scores = (
            jnp.einsum("nqhd,nkhd->nhqk", query_group, keys, preferred_element_type=jnp.float32)
            * scale
        )
        largest = jnp.max(scores, axis=-1, keepdims=True)
        expo = jnp.exp(scores - largest)
        probs = (expo / jnp.sum(expo, axis=-1, keepdims=True)).astype(jnp.bfloat16)
        result = jnp.einsum("nhqk,nkhd->nqhd", probs, values, preferred_element_type=jnp.float32)
        return result.astype(jnp.bfloat16)

    grouped_q = queries.reshape(block_count // group_blocks, group_blocks, BLK, per_device, HD)
    grouped_l = local_lists.reshape(block_count // group_blocks, group_blocks, NBR)
    attended = lax.map(attend, (grouped_q, grouped_l)).reshape(slab_rows, per_device, HD)
    returned = lax.all_to_all(attended, "head", split_axis=0, concat_axis=1, tiled=True)
    flat = returned.reshape(local_rows, HEADS * HD)
    full_out = lax.all_gather(w_out, "seq", axis=0, tiled=True)
    update = jnp.dot(flat, full_out, preferred_element_type=jnp.float32)
    return update.astype(jnp.bfloat16)


def solution(mesh):
    return jax.shard_map(
        local,
        mesh=mesh,
        in_specs=(P(("seq", "head"), None), P("seq", None), P("seq", None), P("seq", None)),
        out_specs=P(("seq", "head"), None),
        check_vma=False,
    )
```

profile of v0, /device:TPU:33, one launch (start us, length us, event | category | flops | bytes accessed | tf_op | source)
XLA Modules:
  0.0 384.4 jit_solution(7192390426923187747)
XLA Ops:
  7.3 71.2 %all-gather.3.cloned.1.call-done = bf16[1024,3072]{1,0:T(8,128)(2,1)} async-done(((bf16[32,3072]{1,0:T(8,128)(2,1)}), bf16[1024,3072]{1,0:T(8,128)(2,1)}) %all-gather.3.cloned.1.call-update) | async-done | bytes 6291472 | tf_op jit(solution)/shard_map/all_gather | solution.py:36
  78.5 6.4 %fusion.29 = bf16[64,8,24,128]{3,1,2,0:T(8,128)(2,1)S(1)} fusion(bf16[512,1024]{1,0:T(8,128)(2,1)S(1)} %copy-done, bf16[1024,3072]{1,0:T(8,128)(2,1)} %all-gather.3.cloned.1.call-done), kind=kOutput, calls=%fused_computation.27 | convolution fusion | flops 3222798336 | bytes 10485760 | tf_op jit(solution)/shard_map/dot_general | solution.py:37
  86.5 82.3 %all_to_all.33 = bf16[512,3,8,128]{3,0,1,2:T(8,128)(2,1)S(1)} all-to-all(bf16[512,3,8,128]{3,0,1,2:T(8,128)(2,1)S(1)} %copy.20), channel_id=1, replica_groups=mesh['seq'=32,'head'=8] {'head'}, dimensions={2} | all-to-all | bytes 6291456 | tf_op jit(solution)/shard_map/all_to_all | solution.py:39
  169.1 1.6 copy-done.1
  171.9 2.4 collective-permute-start
  174.4 1.7 slice.29
  176.2 2.3 slice.31
  178.5 16.8 %collective-permute-done = bf16[2048,2,1,128]{3,0,1,2:T(8,128)(2,1)} collective-permute-done((bf16[2048,2,1,128]{3,0,1,2:T(8,128)(2,1)}, bf16[2048,2,1,128]{3,0,1,2:T(8,128)(2,1)}, u32[]{:S(2)}, u32[]{:S(2)}) %collective-permute-start) | collective-permute-done | bytes 1048608 | tf_op jit(solution)/shard_map/ppermute | solution.py:21
  195.2 8.9 %collective-permute-done.1 = bf16[2048,2,1,128]{3,0,1,2:T(8,128)(2,1)} collective-permute-done((bf16[2048,2,1,128]{3,0,1,2:T(8,128)(2,1)S(1)}, bf16[2048,2,1,128]{3,0,1,2:T(8,128)(2,1)}, u32[]{:S(2)}, u32[]{:S(2)}) %collective-permute-start.1) | collective-permute-done | bytes 1048608 | tf_op jit(solution)/shard_map/ppermute | solution.py:23
  204.2 1.7 pad_maximum_fusion
  205.9 2.2 copy.22
  208.1 123.6 %while.10 = (s32[]{:T(128)}, bf16[8,4,128,1,128]{4,2,1,0,3:T(8,128)(2,1)S(1)}, s32[8,4,12]{2,1,0:T(4,128)S(1)}, bf16[64,128,2,1,128]{4,1,3,2,0:T(8,128)(2,1)}, bf16[8,4,128,1,128]{4,2,1,3,0:T(8,128)(2,1)}, /*index=5*/s32[]{:T(128)}) while((s32[]{:T(128)}, bf16[8,4,128,1,128]{4,2,1,0,3:T(8,128)(2,1)S(1)}, s32[8,4,12]{2,1,0:T(4,128)S(1)}, ...), condition=%wide.region_3.4_spmd, body=%wide.region_0.3_spmd.sunk | while | flops 609555072 | bytes 18229452 | solution.py:67
  208.2 4.9 %gather_fusion = bf16[48,128,2,128]{3,1,2,0:T(8,128)(2,1)} fusion(bf16[64,128,2,128]{3,1,2,0:T(8,128)(2,1)} %bitcast.87, s32[1024]{0:T(1024)S(1)} %pad_clamp_fusion.2), kind=kCustom, calls=%fused_computation.clone.1 | custom fusion | bytes 6291648 | tf_op jit(solution)/shard_map/while/body/eval_jaxpr/gather | solution.py:52
  213.2 4.0 %copy.35 = bf16[48,128,2,128]{3,1,0,2:T(8,128)(2,1)} copy(bf16[48,128,2,128]{3,1,2,0:T(8,128)(2,1)} %gather_fusion) | data formatting | bytes 6291456 | tf_op jit(solution)/shard_map/while/body/eval_jaxpr/gather | solution.py:52
  217.2 2.6 fusion.45
  219.8 3.7 fusion.46
  223.7 4.9 %gather_fusion = bf16[48,128,2,128]{3,1,2,0:T(8,128)(2,1)} fusion(bf16[64,128,2,128]{3,1,2,0:T(8,128)(2,1)} %bitcast.87, s32[1024]{0:T(1024)S(1)} %pad_clamp_fusion.2), kind=kCustom, calls=%fused_computation.clone.1 | custom fusion | bytes 6291648 | tf_op jit(solution)/shard_map/while/body/eval_jaxpr/gather | solution.py:52
  228.7 4.0 %copy.35 = bf16[48,128,2,128]{3,1,0,2:T(8,128)(2,1)} copy(bf16[48,128,2,128]{3,1,2,0:T(8,128)(2,1)} %gather_fusion) | data formatting | bytes 6291456 | tf_op jit(solution)/shard_map/while/body/eval_jaxpr/gather | solution.py:52
  232.7 2.6 fusion.45
  235.2 3.6 fusion.46
  239.2 4.9 %gather_fusion = bf16[48,128,2,128]{3,1,2,0:T(8,128)(2,1)} fusion(bf16[64,128,2,128]{3,1,2,0:T(8,128)(2,1)} %bitcast.87, s32[1024]{0:T(1024)S(1)} %pad_clamp_fusion.2), kind=kCustom, calls=%fused_computation.clone.1 | custom fusion | bytes 6291648 | tf_op jit(solution)/shard_map/while/body/eval_jaxpr/gather | solution.py:52
  244.1 4.0 %copy.35 = bf16[48,128,2,128]{3,1,0,2:T(8,128)(2,1)} copy(bf16[48,128,2,128]{3,1,2,0:T(8,128)(2,1)} %gather_fusion) | data formatting | bytes 6291456 | tf_op jit(solution)/shard_map/while/body/eval_jaxpr/gather | solution.py:52
  248.1 2.6 fusion.45
  250.7 3.6 fusion.46
  254.6 4.9 %gather_fusion = bf16[48,128,2,128]{3,1,2,0:T(8,128)(2,1)} fusion(bf16[64,128,2,128]{3,1,2,0:T(8,128)(2,1)} %bitcast.87, s32[1024]{0:T(1024)S(1)} %pad_clamp_fusion.2), kind=kCustom, calls=%fused_computation.clone.1 | custom fusion | bytes 6291648 | tf_op jit(solution)/shard_map/while/body/eval_jaxpr/gather | solution.py:52
  259.5 4.0 %copy.35 = bf16[48,128,2,128]{3,1,0,2:T(8,128)(2,1)} copy(bf16[48,128,2,128]{3,1,2,0:T(8,128)(2,1)} %gather_fusion) | data formatting | bytes 6291456 | tf_op jit(solution)/shard_map/while/body/eval_jaxpr/gather | solution.py:52
  263.6 2.6 fusion.45
  266.1 3.6 fusion.46
  270.1 4.9 %gather_fusion = bf16[48,128,2,128]{3,1,2,0:T(8,128)(2,1)} fusion(bf16[64,128,2,128]{3,1,2,0:T(8,128)(2,1)} %bitcast.87, s32[1024]{0:T(1024)S(1)} %pad_clamp_fusion.2), kind=kCustom, calls=%fused_computation.clone.1 | custom fusion | bytes 6291648 | tf_op jit(solution)/shard_map/while/body/eval_jaxpr/gather | solution.py:52
  275.0 4.0 %copy.35 = bf16[48,128,2,128]{3,1,0,2:T(8,128)(2,1)} copy(bf16[48,128,2,128]{3,1,2,0:T(8,128)(2,1)} %gather_fusion) | data formatting | bytes 6291456 | tf_op jit(solution)/shard_map/while/body/eval_jaxpr/gather | solution.py:52
  279.0 2.6 fusion.45
  281.6 3.6 fusion.46
  285.5 4.9 %gather_fusion = bf16[48,128,2,128]{3,1,2,0:T(8,128)(2,1)} fusion(bf16[64,128,2,128]{3,1,2,0:T(8,128)(2,1)} %bitcast.87, s32[1024]{0:T(1024)S(1)} %pad_clamp_fusion.2), kind=kCustom, calls=%fused_computation.clone.1 | custom fusion | bytes 6291648 | tf_op jit(solution)/shard_map/while/body/eval_jaxpr/gather | solution.py:52
  290.4 4.0 %copy.35 = bf16[48,128,2,128]{3,1,0,2:T(8,128)(2,1)} copy(bf16[48,128,2,128]{3,1,2,0:T(8,128)(2,1)} %gather_fusion) | data formatting | bytes 6291456 | tf_op jit(solution)/shard_map/while/body/eval_jaxpr/gather | solution.py:52
  294.4 2.6 fusion.45
  297.0 3.6 fusion.46
  300.9 4.9 %gather_fusion = bf16[48,128,2,128]{3,1,2,0:T(8,128)(2,1)} fusion(bf16[64,128,2,128]{3,1,2,0:T(8,128)(2,1)} %bitcast.87, s32[1024]{0:T(1024)S(1)} %pad_clamp_fusion.2), kind=kCustom, calls=%fused_computation.clone.1 | custom fusion | bytes 6291648 | tf_op jit(solution)/shard_map/while/body/eval_jaxpr/gather | solution.py:52
  305.9 4.0 %copy.35 = bf16[48,128,2,128]{3,1,0,2:T(8,128)(2,1)} copy(bf16[48,128,2,128]{3,1,2,0:T(8,128)(2,1)} %gather_fusion) | data formatting | bytes 6291456 | tf_op jit(solution)/shard_map/while/body/eval_jaxpr/gather | solution.py:52
  309.9 2.6 fusion.45
  312.5 3.6 fusion.46
  316.4 4.9 %gather_fusion = bf16[48,128,2,128]{3,1,2,0:T(8,128)(2,1)} fusion(bf16[64,128,2,128]{3,1,2,0:T(8,128)(2,1)} %bitcast.87, s32[1024]{0:T(1024)S(1)} %pad_clamp_fusion.2), kind=kCustom, calls=%fused_computation.clone.1 | custom fusion | bytes 6291648 | tf_op jit(solution)/shard_map/while/body/eval_jaxpr/gather | solution.py:52
  321.3 4.0 %copy.35 = bf16[48,128,2,128]{3,1,0,2:T(8,128)(2,1)} copy(bf16[48,128,2,128]{3,1,2,0:T(8,128)(2,1)} %gather_fusion) | data formatting | bytes 6291456 | tf_op jit(solution)/shard_map/while/body/eval_jaxpr/gather | solution.py:52
  325.3 2.6 fusion.45
  327.9 3.6 fusion.46
  334.0 32.8 %all_to_all.34 = bf16[8,2,32768]{2,1,0:T(2,128)(2,1)} all-to-all(bf16[8,2,32768]{2,1,0:T(2,128)(2,1)S(1)} %reshape.97), channel_id=1, replica_groups=mesh['seq'=32,'head'=8] {'head'}, dimensions={0} | all-to-all | bytes 2097152 | tf_op jit(solution)/shard_map/all_to_all | solution.py:68
  366.8 4.3 %reshape.98 = bf16[4096,1,128]{2,1,0:T(2,128)(2,1)S(1)} reshape(bf16[8,2,32768]{2,1,0:T(2,128)(2,1)} %all_to_all.34) | data formatting | bytes 2097152
  372.2 1.5 copy.26
  373.7 3.8 convolution_convert_fusion.1
  (62 shorter events, 9.2 us)
Async XLA Ops:
  6.5 71.9 %copy-start = (bf16[512,1024]{1,0:T(8,128)(2,1)S(1)}, bf16[512,1024]{1,0:T(8,128)(2,1)}, u32[]{:S(2)}) copy-start(bf16[512,1024]{1,0:T(8,128)(2,1)} %param.6) | copy-start | bytes 3145732
  6.5 71.9 %all-gather.3.cloned.1.call-start = ((), (), s32[]{:S(2)}) async-start(), calls=%async_computation.2 | async-start | bytes 6488064 | tf_op jit(solution)/shard_map/all_gather | solution.py:36
  7.3 366.5 %all-gather.5.cloned.1.call-start = ((), (), s32[]{:S(2)}) async-start(), calls=%async_computation.3 | async-start | bytes 2162688 | tf_op jit(solution)/shard_map/all_gather | solution.py:70
  169.1 1.7 copy-start.1
  169.1 5.2 %copy-start.2 = (s32[32,12]{0,1:T(8,128)S(1)}, s32[32,12]{0,1:T(8,128)}, u32[]{:S(2)}) copy-start(s32[32,12]{0,1:T(8,128)} %param.9) | copy-start | bytes 4612
  171.9 23.4 %collective-permute-start = (bf16[2048,2,1,128]{3,0,1,2:T(8,128)(2,1)}, bf16[2048,2,1,128]{3,0,1,2:T(8,128)(2,1)}, u32[]{:S(2)}, u32[]{:S(2)}) collective-permute-start(bf16[2048,2,1,128]{3,0,1,2:T(8,128)(2,1)} %get-tuple-element.53), channel_id=1, source_target_pairs={{0,8},{8,16},{16,24},{24,32},{32,40},{40,48},{48,56},{56,64},{64,7... | collective-permute-start | bytes 3145736 | tf_op jit(solution)/shard_map/ppermute | solution.py:21
  174.3 29.9 %collective-permute-start.1 = (bf16[2048,2,1,128]{3,0,1,2:T(8,128)(2,1)S(1)}, bf16[2048,2,1,128]{3,0,1,2:T(8,128)(2,1)}, u32[]{:S(2)}, u32[]{:S(2)}) collective-permute-start(bf16[2048,2,1,128]{3,0,1,2:T(8,128)(2,1)S(1)} %get-tuple-element.54), channel_id=1, source_target_pairs={{8,0},{16,8},{24,16},{32,24},{40,32},{48,40},{56,48},{64,56},{72,6... | collective-permute-start | bytes 3145736 | tf_op jit(solution)/shard_map/ppermute | solution.py:23
Sparse Core Ops, SparseCore 0:
  9.2 69.2 all-gather.2
  174.4 60.0 all-gather.4
where the time goes:
time: 386 us; the launch traced here: 384 us
  blocking collectives  115 us (30%)
  waiting for transfers between devices  97.6 us (25%)
  local copies, waits for them, and re-layouts  92.1 us (24%)
  matrix products  59.9 us (16%)
  between operations  13.5 us (3%)
    all_to_all x1, blocking collectives, local(): lax.all_to_all(projected, 'head', split_axis=2, concat_axis=0, tiled=True)  82.3 us
    gather x16, local copies, waits for them, and re-layouts, attend(): kv_blocks[list_group].reshape(group_blocks, NBR * BLK, 2, per_device, HD)  71.6 us
    all_gather x1, waiting for transfers between devices, local(): full_qkv = lax.all_gather(w_qkv, 'seq', axis=0, tiled=True)  71.2 us
    all_to_all x1, blocking collectives, local(): lax.all_to_all(attended, 'head', split_axis=0, concat_axis=1, tiled=True)  32.8 us
    dot_general x8, matrix products, attend(): jnp.einsum('nhqk,nkhd->nqhd', probs, values, preferred_element_type=jnp.f...  29.2 us
    sub x8, matrix products, attend(): expo = jnp.exp(scores - largest)  20.5 us
    ppermute x1, waiting for transfers between devices, padded_2(): lax.ppermute(tail, axis, [(i, (i + 1) % count) for i in range(count)])  16.8 us
    ppermute x1, waiting for transfers between devices, padded_2(): lax.ppermute(head, axis, [((i + 1) % count, i) for i in range(count)])  8.94 us
  transfers between devices with their start and end apart: 4, of which 3 were waited for; matrix products, arithmetic and copies ran while one was open for 37% of the time, Pallas kernels for 0%

commit v1 on v0

--- a/solution.py
+++ b/solution.py
@@ -9,6 +9,12 @@
 BLK = 128
 NBR = 12
 PB = 16
+
+
+def stacked_exchange(x, mesh_axis, split, join):
+    pieces = jnp.split(x, lax.axis_size(mesh_axis), axis=split)
+    received = lax.all_to_all(jnp.stack(pieces), mesh_axis, 0, 0)
+    return jnp.concatenate(received, axis=join)
 
 
 def padded_2(cells, sides, width):
@@ -36,7 +42,7 @@
     full_qkv = lax.all_gather(w_qkv, "seq", axis=0, tiled=True)
     projected = jnp.dot(tokens, full_qkv, preferred_element_type=jnp.float32)
     projected = projected.astype(jnp.bfloat16).reshape(local_rows, 3, HEADS, HD)
-    slab = lax.all_to_all(projected, "head", split_axis=2, concat_axis=0, tiled=True)
+    slab = stacked_exchange(projected, "head", 2, 0)
     queries = slab[:, 0]
     key_value = slab[:, 1:3]
     padded = padded_2(key_value, (("seq", 0),), PB * BLK)

time: 386 us -> 391 us (1.013)
  local copies, waits for them, and re-layouts: 92.1 us -> 97.8 us
    split x0 -> x1, local copies, waits for them, and re-layouts: none -> 5.72 us  [stacked_exchange(): pieces = jnp.split(x, lax.axis_size(mesh_axis), axis=split)]
    unnamed x10 -> x17, local copies, waits for them, and re-layouts: 8.19 us -> 8.83 us
  transfers between devices with their start and end apart: 4 -> 4, of which waited for: 3 -> 3; matrix products, arithmetic and copies ran while one was open for 37% -> 36% of each run, Pallas kernels for 0% -> 0%
where the time goes in v1:
time: 391 us; the launch traced here: 390 us
  blocking collectives  115 us (29%)
  local copies, waits for them, and re-layouts  97.8 us (25%)
  waiting for transfers between devices  97.6 us (25%)
  matrix products  59.9 us (15%)
  between operations  13.6 us (3%)
    all_to_all x1, blocking collectives, stacked_exchange(): received = lax.all_to_all(jnp.stack(pieces), mesh_axis, 0, 0)  82.3 us
    gather x16, local copies, waits for them, and re-layouts, attend(): kv_blocks[list_group].reshape(group_blocks, NBR * BLK, 2, per_device, HD)  71.5 us
    all_gather x1, waiting for transfers between devices, local(): full_qkv = lax.all_gather(w_qkv, 'seq', axis=0, tiled=True)  71.2 us
    all_to_all x1, blocking collectives, local(): lax.all_to_all(attended, 'head', split_axis=0, concat_axis=1, tiled=True)  32.9 us
    dot_general x8, matrix products, attend(): jnp.einsum('nhqk,nkhd->nqhd', probs, values, preferred_element_type=jnp.f...  29.1 us
    sub x8, matrix products, attend(): expo = jnp.exp(scores - largest)  20.5 us
    ppermute x1, waiting for transfers between devices, padded_2(): lax.ppermute(tail, axis, [(i, (i + 1) % count) for i in range(count)])  16.7 us
    ppermute x1, waiting for transfers between devices, padded_2(): lax.ppermute(head, axis, [((i + 1) % count, i) for i in range(count)])  8.94 us
  transfers between devices with their start and end apart: 4, of which 3 were waited for; matrix products, arithmetic and copies ran while one was open for 36% of the time, Pallas kernels for 0%

profile of v1, /device:TPU:33, one launch (start us, length us, event | category | flops | bytes accessed | tf_op | source)
XLA Modules:
  0.0 390.2 jit_solution(3341953515791425075)
XLA Ops:
  7.3 71.2 %all-gather.3.cloned.1.call-done = bf16[1024,3072]{1,0:T(8,128)(2,1)} async-done(((bf16[32,3072]{1,0:T(8,128)(2,1)}), bf16[1024,3072]{1,0:T(8,128)(2,1)}) %all-gather.3.cloned.1.call-update) | async-done | bytes 6291472 | tf_op jit(solution)/shard_map/all_gather | solution.py:42
  78.5 6.4 %fusion.29 = bf16[64,8,24,128]{3,1,2,0:T(8,128)(2,1)S(1)} fusion(bf16[512,1024]{1,0:T(8,128)(2,1)S(1)} %copy-done, bf16[1024,3072]{1,0:T(8,128)(2,1)} %all-gather.3.cloned.1.call-done), kind=kOutput, calls=%fused_computation.27 | convolution fusion | flops 3222798336 | bytes 10485760 | tf_op jit(solution)/shard_map/dot_general | solution.py:43
  85.8 5.7 %fusion.43 = (bf16[512,3,1,128]{3,2,1,0:T(2,128)(2,1)S(1)}, bf16[512,3,1,128]{3,2,1,0:T(2,128)(2,1)S(1)}, bf16[512,3,1,128]{3,2,1,0:T(2,128)(2,1)S(1)}, bf16[512...) fusion(bf16[512,3,8,128]{3,2,1,0:T(8,128)(2,1)S(1)} %bitcast.118), kind=kLoop, calls=%fused_computation.51 | loop fusion | bytes 6291456 | tf_op jit(solution)/shard_map/split | solution.py:15
  92.3 82.3 %all_to_all.20 = bf16[8,512,3,1,128]{4,1,3,2,0:T(8,128)(2,1)S(1)} all-to-all(bf16[8,512,3,1,128]{4,1,3,2,0:T(8,128)(2,1)S(1)} %fusion.30), channel_id=1, replica_groups=mesh['seq'=32,'head'=8] {'head'}, dimensions={0} | all-to-all | bytes 6291456 | tf_op jit(solution)/shard_map/all_to_all | solution.py:16
  175.0 1.6 copy-done.1
  177.7 2.4 collective-permute-start
  180.3 1.7 slice.29
  182.0 2.3 slice.31
  184.4 16.7 %collective-permute-done = bf16[2048,2,1,128]{3,0,1,2:T(8,128)(2,1)} collective-permute-done((bf16[2048,2,1,128]{3,0,1,2:T(8,128)(2,1)}, bf16[2048,2,1,128]{3,0,1,2:T(8,128)(2,1)}, u32[]{:S(2)}, u32[]{:S(2)}) %collective-permute-start) | collective-permute-done | bytes 1048608 | tf_op jit(solution)/shard_map/ppermute | solution.py:27
  201.1 8.9 %collective-permute-done.1 = bf16[2048,2,1,128]{3,0,1,2:T(8,128)(2,1)} collective-permute-done((bf16[2048,2,1,128]{3,0,1,2:T(8,128)(2,1)S(1)}, bf16[2048,2,1,128]{3,0,1,2:T(8,128)(2,1)}, u32[]{:S(2)}, u32[]{:S(2)}) %collective-permute-start.1) | collective-permute-done | bytes 1048608 | tf_op jit(solution)/shard_map/ppermute | solution.py:29
  210.0 1.7 pad_maximum_fusion
  211.7 2.2 copy.59
  214.0 123.5 %while.10 = (s32[]{:T(128)}, bf16[8,4,128,1,128]{4,2,1,0,3:T(8,128)(2,1)S(1)}, s32[8,4,12]{2,1,0:T(4,128)S(1)}, bf16[64,128,2,1,128]{4,1,3,2,0:T(8,128)(2,1)}, bf16[8,4,128,1,128]{4,2,1,3,0:T(8,128)(2,1)}, /*index=5*/s32[]{:T(128)}) while((s32[]{:T(128)}, bf16[8,4,128,1,128]{4,2,1,0,3:T(8,128)(2,1)S(1)}, s32[8,4,12]{2,1,0:T(4,128)S(1)}, ...), condition=%wide.region_3.4_spmd, body=%wide.region_0.3_spmd.sunk | while | flops 609555072 | bytes 18229452 | solution.py:73
  214.1 4.9 %gather_fusion = bf16[48,128,2,128]{3,1,2,0:T(8,128)(2,1)} fusion(bf16[64,128,2,128]{3,1,2,0:T(8,128)(2,1)} %bitcast.115, s32[1024]{0:T(1024)S(1)} %pad_clamp_fusion.2), kind=kCustom, calls=%fused_computation.clone.1 | custom fusion | bytes 6291648 | tf_op jit(solution)/shard_map/while/body/eval_jaxpr/gather | solution.py:58
  219.0 4.0 %copy.104 = bf16[48,128,2,128]{3,1,0,2:T(8,128)(2,1)} copy(bf16[48,128,2,128]{3,1,2,0:T(8,128)(2,1)} %gather_fusion) | data formatting | bytes 6291456 | tf_op jit(solution)/shard_map/while/body/eval_jaxpr/gather | solution.py:58
  223.0 2.6 fusion.54
  225.6 3.7 fusion.55
  229.6 4.9 %gather_fusion = bf16[48,128,2,128]{3,1,2,0:T(8,128)(2,1)} fusion(bf16[64,128,2,128]{3,1,2,0:T(8,128)(2,1)} %bitcast.115, s32[1024]{0:T(1024)S(1)} %pad_clamp_fusion.2), kind=kCustom, calls=%fused_computation.clone.1 | custom fusion | bytes 6291648 | tf_op jit(solution)/shard_map/while/body/eval_jaxpr/gather | solution.py:58
  234.5 4.0 %copy.104 = bf16[48,128,2,128]{3,1,0,2:T(8,128)(2,1)} copy(bf16[48,128,2,128]{3,1,2,0:T(8,128)(2,1)} %gather_fusion) | data formatting | bytes 6291456 | tf_op jit(solution)/shard_map/while/body/eval_jaxpr/gather | solution.py:58
  238.5 2.6 fusion.54
  241.1 3.6 fusion.55
  245.0 4.9 %gather_fusion = bf16[48,128,2,128]{3,1,2,0:T(8,128)(2,1)} fusion(bf16[64,128,2,128]{3,1,2,0:T(8,128)(2,1)} %bitcast.115, s32[1024]{0:T(1024)S(1)} %pad_clamp_fusion.2), kind=kCustom, calls=%fused_computation.clone.1 | custom fusion | bytes 6291648 | tf_op jit(solution)/shard_map/while/body/eval_jaxpr/gather | solution.py:58
  249.9 4.0 %copy.104 = bf16[48,128,2,128]{3,1,0,2:T(8,128)(2,1)} copy(bf16[48,128,2,128]{3,1,2,0:T(8,128)(2,1)} %gather_fusion) | data formatting | bytes 6291456 | tf_op jit(solution)/shard_map/while/body/eval_jaxpr/gather | solution.py:58
  253.9 2.6 fusion.54
  256.5 3.6 fusion.55
  260.4 4.9 %gather_fusion = bf16[48,128,2,128]{3,1,2,0:T(8,128)(2,1)} fusion(bf16[64,128,2,128]{3,1,2,0:T(8,128)(2,1)} %bitcast.115, s32[1024]{0:T(1024)S(1)} %pad_clamp_fusion.2), kind=kCustom, calls=%fused_computation.clone.1 | custom fusion | bytes 6291648 | tf_op jit(solution)/shard_map/while/body/eval_jaxpr/gather | solution.py:58
  265.4 4.0 %copy.104 = bf16[48,128,2,128]{3,1,0,2:T(8,128)(2,1)} copy(bf16[48,128,2,128]{3,1,2,0:T(8,128)(2,1)} %gather_fusion) | data formatting | bytes 6291456 | tf_op jit(solution)/shard_map/while/body/eval_jaxpr/gather | solution.py:58
  269.4 2.6 fusion.54
  271.9 3.6 fusion.55
  275.9 4.9 %gather_fusion = bf16[48,128,2,128]{3,1,2,0:T(8,128)(2,1)} fusion(bf16[64,128,2,128]{3,1,2,0:T(8,128)(2,1)} %bitcast.115, s32[1024]{0:T(1024)S(1)} %pad_clamp_fusion.2), kind=kCustom, calls=%fused_computation.clone.1 | custom fusion | bytes 6291648 | tf_op jit(solution)/shard_map/while/body/eval_jaxpr/gather | solution.py:58
  280.8 4.0 %copy.104 = bf16[48,128,2,128]{3,1,0,2:T(8,128)(2,1)} copy(bf16[48,128,2,128]{3,1,2,0:T(8,128)(2,1)} %gather_fusion) | data formatting | bytes 6291456 | tf_op jit(solution)/shard_map/while/body/eval_jaxpr/gather | solution.py:58
  284.8 2.6 fusion.54
  287.4 3.6 fusion.55
  291.3 4.9 %gather_fusion = bf16[48,128,2,128]{3,1,2,0:T(8,128)(2,1)} fusion(bf16[64,128,2,128]{3,1,2,0:T(8,128)(2,1)} %bitcast.115, s32[1024]{0:T(1024)S(1)} %pad_clamp_fusion.2), kind=kCustom, calls=%fused_computation.clone.1 | custom fusion | bytes 6291648 | tf_op jit(solution)/shard_map/while/body/eval_jaxpr/gather | solution.py:58
  296.2 4.0 %copy.104 = bf16[48,128,2,128]{3,1,0,2:T(8,128)(2,1)} copy(bf16[48,128,2,128]{3,1,2,0:T(8,128)(2,1)} %gather_fusion) | data formatting | bytes 6291456 | tf_op jit(solution)/shard_map/while/body/eval_jaxpr/gather | solution.py:58
  300.2 2.6 fusion.54
  302.8 3.6 fusion.55
  306.7 4.9 %gather_fusion = bf16[48,128,2,128]{3,1,2,0:T(8,128)(2,1)} fusion(bf16[64,128,2,128]{3,1,2,0:T(8,128)(2,1)} %bitcast.115, s32[1024]{0:T(1024)S(1)} %pad_clamp_fusion.2), kind=kCustom, calls=%fused_computation.clone.1 | custom fusion | bytes 6291648 | tf_op jit(solution)/shard_map/while/body/eval_jaxpr/gather | solution.py:58
  311.7 4.0 %copy.104 = bf16[48,128,2,128]{3,1,0,2:T(8,128)(2,1)} copy(bf16[48,128,2,128]{3,1,2,0:T(8,128)(2,1)} %gather_fusion) | data formatting | bytes 6291456 | tf_op jit(solution)/shard_map/while/body/eval_jaxpr/gather | solution.py:58
  315.7 2.6 fusion.54
  318.2 3.6 fusion.55
  322.2 4.9 %gather_fusion = bf16[48,128,2,128]{3,1,2,0:T(8,128)(2,1)} fusion(bf16[64,128,2,128]{3,1,2,0:T(8,128)(2,1)} %bitcast.115, s32[1024]{0:T(1024)S(1)} %pad_clamp_fusion.2), kind=kCustom, calls=%fused_computation.clone.1 | custom fusion | bytes 6291648 | tf_op jit(solution)/shard_map/while/body/eval_jaxpr/gather | solution.py:58
  327.1 4.0 %copy.104 = bf16[48,128,2,128]{3,1,0,2:T(8,128)(2,1)} copy(bf16[48,128,2,128]{3,1,2,0:T(8,128)(2,1)} %gather_fusion) | data formatting | bytes 6291456 | tf_op jit(solution)/shard_map/while/body/eval_jaxpr/gather | solution.py:58
  331.1 2.6 fusion.54
  333.7 3.6 fusion.55
  339.7 32.9 %all_to_all.21 = bf16[8,2,32768]{2,1,0:T(2,128)(2,1)} all-to-all(bf16[8,2,32768]{2,1,0:T(2,128)(2,1)S(1)} %reshape.101), channel_id=1, replica_groups=mesh['seq'=32,'head'=8] {'head'}, dimensions={0} | all-to-all | bytes 2097152 | tf_op jit(solution)/shard_map/all_to_all | solution.py:74
  372.6 4.3 %reshape.102 = bf16[4096,1,128]{2,1,0:T(2,128)(2,1)S(1)} reshape(bf16[8,2,32768]{2,1,0:T(2,128)(2,1)} %all_to_all.21) | data formatting | bytes 2097152
  379.5 3.8 convolution_convert_fusion.1
  (70 shorter events, 10.8 us)
Async XLA Ops:
  6.5 71.9 %copy-start = (bf16[512,1024]{1,0:T(8,128)(2,1)S(1)}, bf16[512,1024]{1,0:T(8,128)(2,1)}, u32[]{:S(2)}) copy-start(bf16[512,1024]{1,0:T(8,128)(2,1)} %param.6) | copy-start | bytes 3145732
  6.5 71.9 %all-gather.3.cloned.1.call-start = ((), (), s32[]{:S(2)}) async-start(), calls=%async_computation.2 | async-start | bytes 6488064 | tf_op jit(solution)/shard_map/all_gather | solution.py:42
  7.3 372.3 %all-gather.5.cloned.1.call-start = ((), (), s32[]{:S(2)}) async-start(), calls=%async_computation.3 | async-start | bytes 2162688 | tf_op jit(solution)/shard_map/all_gather | solution.py:76
  175.0 1.7 copy-start.1
  175.0 5.2 %copy-start.2 = (s32[32,12]{0,1:T(8,128)S(1)}, s32[32,12]{0,1:T(8,128)}, u32[]{:S(2)}) copy-start(s32[32,12]{0,1:T(8,128)} %param.9) | copy-start | bytes 4612
  177.7 23.4 %collective-permute-start = (bf16[2048,2,1,128]{3,0,1,2:T(8,128)(2,1)}, bf16[2048,2,1,128]{3,0,1,2:T(8,128)(2,1)}, u32[]{:S(2)}, u32[]{:S(2)}) collective-permute-start(bf16[2048,2,1,128]{3,0,1,2:T(8,128)(2,1)} %get-tuple-element.58), channel_id=1, source_target_pairs={{0,8},{8,16},{16,24},{24,32},{32,40},{40,48},{48,56},{56,64},{64,7... | collective-permute-start | bytes 3145736 | tf_op jit(solution)/shard_map/ppermute | solution.py:27
  180.1 29.9 %collective-permute-start.1 = (bf16[2048,2,1,128]{3,0,1,2:T(8,128)(2,1)S(1)}, bf16[2048,2,1,128]{3,0,1,2:T(8,128)(2,1)}, u32[]{:S(2)}, u32[]{:S(2)}) collective-permute-start(bf16[2048,2,1,128]{3,0,1,2:T(8,128)(2,1)S(1)} %get-tuple-element.59), channel_id=1, source_target_pairs={{8,0},{16,8},{24,16},{32,24},{40,32},{48,40},{56,48},{64,56},{72,6... | collective-permute-start | bytes 3145736 | tf_op jit(solution)/shard_map/ppermute | solution.py:29
Sparse Core Ops, SparseCore 0:
  9.2 69.2 all-gather.2
  180.3 60.0 all-gather.4
